TPU v7x, 32 devices: a whole 2x2x4 slice. The times are simulated.
32 devices in a mesh: grp: 2 (over x), row: 16 (over z, y, core).
Axes of the slice: x: 2, y: 2, z: 4, core: 2. Of those that a mesh axis runs over, the one named last changes fastest.
Arguments:
- excitations: bfloat16 [32, 8192, 128], P('grp', 'row'), parts along dimension 0, may hold values from -0.005859375 to 0.005859375
- valence_orb: bfloat16 [2048, 128], P(('grp', 'row')), parts along dimension 0, may hold values from -6 to 6
- conduction_orb: bfloat16 [2048, 8192], P(('grp', 'row')), parts along dimension 0, may hold values from -6 to 6
- screened: bfloat16 [2048, 1024], P(('grp', 'row')), parts along dimension 0, may hold values from -0.005859375 to 0.005859375
Outputs:
- action: bfloat16 [32, 8192, 128], P('grp', 'row'), parts along dimension 0
There are 2 independent parts, one for each index of `grp`. A program takes and returns all parts, laid end to end along the dimension named above; each array names one. Nothing has to cross between parts.
All inputs are finite; a program needn't handle non-finite values.
Results may differ from a plain program's by a relative error of at most 0.0064.
Values may be sent and summed in bfloat16 or wider, within the bound.
A program may use at most 64 MiB of HBM per device.

v0:
```python
import functools
import math

import jax
import jax.numpy as jnp
from jax import lax
from jax.experimental import pallas as pl
from jax.experimental.pallas import tpu as pltpu
from jax.sharding import PartitionSpec as P

MESH = pl.DeviceIdType.MESH
NT = (((1,), (1,)), ((), ()))


def flip(index, other, bits):
    total = 0
    for bit in range(bits):
        a = (index // (1 << bit)) % 2
        b = (other // (1 << bit)) % 2
        total = total + (a + b - 2 * a * b) * (1 << bit)
    return total


def send_order(n, q):
    far = list(range(n - 1, n // 2 - 1, -1))
    near = [1] + [k for k in range(n // 2 - 1, 1, -1) if k // 2 != q // 4]
    near[3:3] = [k for k in range(n // 2 - 1, 1, -1) if k // 2 == q // 4]
    order = []
    while far or near:
        order += far[:2] + near[:3]
        far, near = far[2:], near[3:]
    return order


def work_order(n, q):
    seen, order = {0}, [0]
    for k in send_order(n, q):
        seen.add(k)
        if seen >= {k, k ^ 1} and k // 2 not in order:
            order.append(k // 2)
    return order


def gather_kernel(
    n, planes,
    exc_hbm, val_ref, cond_hbm, scr_ref,
    condt_hbm, valt_hbm, field_hbm,
    condt_ref, valt_ref, field_ref, exc, exct, cond_all, val_all, scr_chip, part, red, dens, dens_all, fld, fld_all,
    exc_sem, own_sem, out_sem, field_sem,
    cond_send, cond_recv, scr_send, scr_recv, va_send, va_recv, vb_send, vb_recv,
    part_send, part_recv, dens_send, dens_recv, fld_send, fld_recv,
):
    rows, cl = val_ref.shape[0], exc.shape[1]
    batch = exc.shape[0]
    half = batch // 2
    q = n // planes
    bits = n.bit_length() - 1
    chips = n // 2
    me = lax.axis_index("row")
    my_z, my_q = me // q, me % q
    chip, core = me // 2, me % 2

    exc_copy = pltpu.make_async_copy(exc_hbm, exc, exc_sem)
    exc_copy.start()
    own_val = pltpu.make_async_copy(val_ref, val_all.at[my_q, my_z], own_sem.at[0])
    own_val.start()
    own_scr = pltpu.make_async_copy(scr_ref, scr_chip.at[core], own_sem.at[1])
    own_scr.start()
    pltpu.make_async_copy(
        cond_hbm.at[:, pl.ds(pl.multiple_of(me * cl, cl), cl)], cond_all.at[me], cond_recv.at[me]
    ).start()

    barrier = pltpu.get_barrier_semaphore()
    for k in range(1, n):
        pl.semaphore_signal(barrier, inc=1, device_id={"row": flip(me, k, bits)}, device_id_type=MESH)
    pl.semaphore_wait(barrier, n - 1)

    def remote(src, dst, send, recv, to):
        return pltpu.make_async_remote_copy(
            src_ref=src, dst_ref=dst, send_sem=send, recv_sem=recv,
            device_id={"row": to}, device_id_type=MESH,
        )

    sent = []
    zbits, qbits = planes.bit_length() - 1, q.bit_length() - 1
    for k in range(planes - 1, 0, -1):
        to = flip(my_z, k, zbits) * q + my_q
        copy = remote(val_ref, val_all.at[my_q, my_z], va_send.at[k], va_recv.at[my_z], to)
        copy.start()
        sent.append(copy)
    for k in send_order(n, q):
        to = flip(me, k, bits)
        copy = remote(
            cond_hbm.at[:, pl.ds(pl.multiple_of(to * cl, cl), cl)], cond_all.at[me],
            cond_send.at[k], cond_recv.at[me], to,
        )
        copy.start()
        sent.append(copy)
    copy = remote(scr_ref, scr_chip.at[core], scr_send, scr_recv, chip * 2 + 1 - core)
    copy.start()
    sent.append(copy)

    exc_copy.wait()

    def turn(b, carry):
        exct[pl.ds(pl.multiple_of(b * 128, 128), 128), :] = exc[b].T
        return carry

    lax.fori_loop(0, batch, turn, 0)

    own_val.wait()
    for k in range(1, planes):
        z = flip(my_z, k, zbits)
        pltpu.make_async_copy(val_ref, val_all.at[my_q, z], va_recv.at[z]).wait()
    for k in range(1, q):
        to = my_z * q + flip(my_q, k, qbits)
        copy = remote(val_all.at[my_q], val_all.at[my_q], vb_send.at[k], vb_recv.at[my_q], to)
        copy.start()
        sent.append(copy)
    for k in range(1, q):
        other = flip(my_q, k, qbits)
        pltpu.make_async_copy(val_all.at[other], val_all.at[other], vb_recv.at[other]).wait()

    def group(step, carry):
        k = 0
        for at, value in enumerate(work_order(n, q)):
            k = k + jnp.where(step == at, value, 0)
        p = flip(chip, k, bits - 1)
        z, y = p // (q // 2), p % (q // 2)
        lanes = pl.ds(pl.multiple_of(p * 2 * rows, 2 * rows), 2 * rows)
        for h in range(2):
            pltpu.make_async_copy(cond_all.at[2 * p + h], cond_all.at[2 * p + h], cond_recv.at[2 * p + h]).wait()
        block = cond_all[pl.ds(2 * p, 2)].reshape(2 * rows, cl)
        vals = jnp.concatenate([val_all[2 * y, z], val_all[2 * y + 1, z]], axis=0)
        valt = vals.astype(jnp.float32).T
        valt_ref[:, lanes] = valt.astype(jnp.bfloat16)
        mixed = lax.dot_general(exct[...], block, NT, preferred_element_type=jnp.float32)
        summed = jnp.sum(mixed.reshape(batch, valt.shape[0], 2 * rows) * valt[None], axis=1)
        part[k, 0] = summed[:half]
        part[k, 1] = summed[half:]

        @pl.when(k == 0)
        def _():
            remote(
                part.at[k, 1 - core], red.at[me], part_send.at[k, 1 - core], part_recv.at[me],
                2 * chip + 1 - core,
            ).start()
            red[me] = part[0, core]

        @pl.when(k > 0)
        def _():
            for h in range(2):
                remote(
                    part.at[k, h], red.at[me], part_send.at[k, h], part_recv.at[me], 2 * p + h
                ).start()

        condt_ref[:, lanes] = block.T
        pltpu.make_async_copy(condt_ref.at[:, lanes], condt_hbm.at[:, lanes], out_sem.at[k, 0]).start()
        pltpu.make_async_copy(valt_ref.at[:, lanes], valt_hbm.at[:, lanes], out_sem.at[k, 1]).start()
        return carry

    lax.fori_loop(0, chips, group, 0)

    own_scr.wait()
    pltpu.make_async_copy(scr_chip.at[1 - core], scr_chip.at[1 - core], scr_recv).wait()
    total = red[me]
    for k in range(1, n):
        other = flip(me, k, bits)
        pltpu.make_async_copy(red.at[other], red.at[other], part_recv.at[other]).wait()
        total = total + red[other]
    dens[...] = total.astype(jnp.bfloat16)
    dens_all[chip] = total.astype(jnp.bfloat16)
    for k in range(chips - 1, 0, -1):
        to = flip(chip, k, bits - 1)
        copy = remote(dens, dens_all.at[chip], dens_send.at[k], dens_recv.at[chip], 2 * to + core)
        copy.start()
        sent.append(copy)
    for k in range(1, chips):
        other = flip(chip, k, bits - 1)
        pltpu.make_async_copy(dens_all.at[other], dens_all.at[other], dens_recv.at[other]).wait()
    whole = jnp.concatenate([dens_all[p].astype(jnp.float32) for p in range(chips)], axis=1).astype(jnp.bfloat16)
    screened = scr_chip[...].reshape(2 * rows, scr_ref.shape[1])
    mine = lax.dot_general(whole, screened, NT, preferred_element_type=jnp.float32).astype(jnp.bfloat16)
    fld[...] = mine
    fld_all[me] = mine
    for k in range(n - 1, 0, -1):
        copy = remote(fld, fld_all.at[me], fld_send.at[k], fld_recv.at[me], flip(me, k, bits))
        copy.start()
        sent.append(copy)
    for k in range(1, n):
        other = flip(me, k, bits)
        pltpu.make_async_copy(fld_all.at[other], fld_all.at[other], fld_recv.at[other]).wait()
    for p in range(chips):
        for h in range(2):
            field_ref[h * half:(h + 1) * half, p * 2 * rows:(p + 1) * 2 * rows] = fld_all[2 * p + h].astype(jnp.float32)

    field_copy = pltpu.make_async_copy(field_ref, field_hbm, field_sem)
    field_copy.start()
    for k in range(chips):
        lanes = pl.ds(pl.multiple_of(flip(chip, k, bits - 1) * 2 * rows, 2 * rows), 2 * rows)
        pltpu.make_async_copy(condt_ref.at[:, lanes], condt_hbm.at[:, lanes], out_sem.at[k, 0]).wait()
        pltpu.make_async_copy(valt_ref.at[:, lanes], valt_hbm.at[:, lanes], out_sem.at[k, 1]).wait()
    for copy in sent:
        copy.wait_send()
    remote(
        part.at[0, 1 - core], red.at[me], part_send.at[0, 1 - core], part_recv.at[me], 2 * chip + 1 - core
    ).wait_send()
    for k in range(1, chips):
        p = flip(chip, k, bits - 1)
        for h in range(2):
            remote(part.at[k, h], red.at[me], part_send.at[k, h], part_recv.at[me], 2 * p + h).wait_send()
    field_copy.wait()


def project_kernel(condt_hbm, valt_hbm, field_hbm, out_hbm, condt_ref, valt_ref, field_ref, held, in_sem, out_sem):
    loads = [
        pltpu.make_async_copy(src, dst, in_sem.at[at])
        for at, (src, dst) in enumerate(((valt_hbm, valt_ref), (field_hbm, field_ref), (condt_hbm, condt_ref)))
    ]
    for load in loads:
        load.start()
    loads[0].wait()
    loads[1].wait()
    v = valt_ref.shape[0]
    batch = field_ref.shape[0]
    valt = valt_ref[...]
    copies = []
    for b in range(0, batch, 4):
        weights = jnp.concatenate(
            [valt * field_ref[b + i:b + i + 1, :].astype(jnp.bfloat16) for i in range(4)], axis=0
        )
        if b == 0:
            loads[2].wait()
        summed = lax.dot_general(condt_ref[...], weights, NT, preferred_element_type=jnp.float32)
        for i in range(4):
            held[b + i] = summed[:, i * v:(i + 1) * v].astype(jnp.bfloat16)
        copy = pltpu.make_async_copy(held.at[pl.ds(b, 4)], out_hbm.at[pl.ds(b, 4)], out_sem.at[b // 4])
        copy.start()
        copies.append(copy)
    for copy in copies:
        copy.wait()


def fast_body(n, excitations, valence_orb, conduction_orb, screened):
    batch, cl, v = excitations.shape
    rows, points = screened.shape
    planes = 4 if n % 8 == 0 else 2
    q, chips, half = n // planes, n // 2, batch // 2
    bf, f32 = jnp.bfloat16, jnp.float32
    hbm = pl.BlockSpec(memory_space=pltpu.HBM)
    dma = pltpu.SemaphoreType.DMA
    condt, valt, field = pl.pallas_call(
        functools.partial(gather_kernel, n, planes),
        out_shape=(
            jax.ShapeDtypeStruct((cl, points), bf),
            jax.ShapeDtypeStruct((v, points), bf),
            jax.ShapeDtypeStruct((batch, points), f32),
        ),
        in_specs=[hbm, hbm, hbm, hbm],
        out_specs=(hbm, hbm, hbm),
        scratch_shapes=[
            pltpu.VMEM((cl, points), bf),
            pltpu.VMEM((v, points), bf),
            pltpu.VMEM((batch, points), f32),
            pltpu.VMEM((batch, cl, v), bf),
            pltpu.VMEM((batch * v, cl), bf),
            pltpu.VMEM((n, rows, cl), bf),
            pltpu.VMEM((q, planes, rows, v), bf),
            pltpu.VMEM((2, rows, points), bf),
            pltpu.VMEM((chips, 2, half, 2 * rows), f32),
            pltpu.VMEM((n, half, 2 * rows), f32),
            pltpu.VMEM((half, 2 * rows), bf),
            pltpu.VMEM((chips, half, 2 * rows), bf),
            pltpu.VMEM((half, 2 * rows), bf),
            pltpu.VMEM((n, half, 2 * rows), bf),
            dma, dma((2,)), dma((chips, 2)), dma,
            dma((n,)), dma((n,)), dma, dma, dma((planes,)), dma((planes,)), dma((q,)), dma((q,)),
            dma((chips, 2)), dma((n,)), dma((chips,)), dma((chips,)), dma((n,)), dma((n,)),
        ],
        compiler_params=pltpu.CompilerParams(
            collective_id=0, has_side_effects=True, vmem_limit_bytes=63 * 1024 * 1024
        ),
        name="gather_field",
    )(excitations, valence_orb, conduction_orb, screened)
    return pl.pallas_call(
        project_kernel,
        out_shape=jax.ShapeDtypeStruct((batch, cl, v), bf),
        in_specs=[hbm, hbm, hbm],
        out_specs=hbm,
        scratch_shapes=[
            pltpu.VMEM((cl, points), bf), pltpu.VMEM((v, points), bf), pltpu.VMEM((batch, points), f32),
            pltpu.VMEM((batch, cl, v), bf), dma((3,)), dma((batch // 2,))],
        compiler_params=pltpu.CompilerParams(vmem_limit_bytes=63 * 1024 * 1024),
        name="project",
    )(condt, valt, field)


def over_blocks(total_rows, step_fn, initial):
    span_size = math.gcd(total_rows, 2048)
    block_count = total_rows // span_size
    if block_count == 1:
        return step_fn(initial, 0, span_size)
    return lax.fori_loop(
        0, block_count, lambda index, carry: step_fn(carry, index * span_size, span_size), initial
    )


def density_rows(flat_exc, batch, valence_rows, cond_rows):
    total_rows = valence_rows.shape[0]
    cond_local = cond_rows.shape[1]
    initial = jnp.zeros((batch, total_rows), jnp.float32)

    def step_fn(carry, offset, span_size):
        val_block = lax.dynamic_slice_in_dim(valence_rows, offset, span_size, 0)
        cond_block = lax.dynamic_slice_in_dim(cond_rows, offset, span_size, 0)
        mixed = lax.dot_general(
            flat_exc, val_block, (((1,), (1,)), ((), ())), preferred_element_type=jnp.float32
        )
        mixed = mixed.reshape(batch, cond_local, span_size)
        summed = jnp.sum(mixed * cond_block.T.astype(jnp.float32)[None], axis=1)
        return lax.dynamic_update_slice_in_dim(carry, summed, offset, 1)

    return over_blocks(total_rows, step_fn, initial)


def projection(carry, valence_rows, cond_rows, field_cols):
    total_rows = valence_rows.shape[0]
    batch = field_cols.shape[0]
    cond_local = cond_rows.shape[1]

    def step_fn(inner, offset, span_size):
        val_block = lax.dynamic_slice_in_dim(valence_rows, offset, span_size, 0)
        cond_block = lax.dynamic_slice_in_dim(cond_rows, offset, span_size, 0)
        field_block = lax.dynamic_slice_in_dim(field_cols, offset, span_size, 1)
        pair = (
            cond_block.T.astype(jnp.float32)[None] * field_block.astype(jnp.float32)[:, None, :]
        ).astype(jnp.bfloat16)
        pair = pair.reshape(batch * cond_local, span_size)
        return inner + jnp.dot(pair, val_block, preferred_element_type=jnp.float32)

    return over_blocks(total_rows, step_fn, carry)


def general_body(excitations, valence_orb, conduction_orb, screened):
    batch, cond_local, valence = excitations.shape
    flat_exc = excitations.reshape(batch * cond_local, valence)
    valence_whole = lax.all_gather(valence_orb, "row", axis=0, tiled=True)
    cond_rows = lax.all_to_all(conduction_orb, "row", split_axis=1, concat_axis=0, tiled=True)
    partial_density = density_rows(flat_exc, batch, valence_whole, cond_rows)
    density_whole = lax.psum(partial_density, "row").astype(jnp.bfloat16)
    field_mine = lax.dot_general(
        density_whole, screened, (((1,), (1,)), ((), ())), preferred_element_type=jnp.float32
    ).astype(jnp.bfloat16)
    initial = jnp.zeros((batch * cond_local, valence), jnp.float32)
    summed = projection(
        initial, valence_whole, cond_rows, lax.all_gather(field_mine, "row", axis=1, tiled=True)
    )
    return summed.reshape(batch, cond_local, valence).astype(jnp.bfloat16)


def body(n, excitations, valence_orb, conduction_orb, screened):
    batch, cl, v = excitations.shape
    rows = valence_orb.shape[0]
    fits = n in (8, 16) and cl % 128 == 0 and v == 128 and rows == 64 and batch == 16
    if fits:
        return fast_body(n, excitations, valence_orb, conduction_orb, screened)
    return general_body(excitations, valence_orb, conduction_orb, screened)


def solution(mesh):
    in_specs = (
        P("grp", "row", None),
        P(("grp", "row"), None),
        P(("grp", "row"), None),
        P(("grp", "row"), None),
    )
    out_specs = P("grp", "row", None)
    return jax.shard_map(
        functools.partial(body, mesh.shape["row"]),
        mesh=mesh, in_specs=in_specs, out_specs=out_specs, check_vma=False,
    )
```

profile of v0, /device:TPU:0, one launch (start us, length us, event | category | flops | bytes accessed | tf_op | source)
XLA Modules:
  0.0 51.6 jit_solution(5602491273913235114)
XLA Ops:
  0.0 47.0 %gather_field.1 = (bf16[512,1024]{1,0:T(8,128)(2,1)}, bf16[128,1024]{1,0:T(8,128)(2,1)}, f32[16,1024]{1,0:T(8,128)}) custom-call(bf16[16,512,128]{2,1,0:T(8,128)(2,1)} %exc_hbm.1, bf16[64,128]{1,0:T(8,128)(2,1)} %val_ref.1, bf16[64,8192]{1,0:T(8,128)(2,1)} %cond_hbm.1, bf16[64,1024]{1,0:T(8,128)(2,1)} %scr_ref.1), custom_call_target="tpu_custom_call" | custom-call | tf_op jit(solution)/shard_map/gather_field/pallas_call | solution.py:252
  47.0 4.6 %project.1 = bf16[16,512,128]{2,1,0:T(8,128)(2,1)} custom-call(bf16[512,1024]{1,0:T(8,128)(2,1)} %get-tuple-element.8.condt_hbm, bf16[128,1024]{1,0:T(8,128)(2,1)} %get-tuple-element.9.valt_hbm, f32[16,1024]{1,0:T(8,128)} %get-tuple-element.10.field_hbm), custom_call_target="tpu_custom_call" | custom-call | tf_op jit(solution)/shard_map/project/pallas_call | solution.py:285
where the time goes:
time: 51.8 us; the launch traced here: 51.6 us
  Pallas kernels  51.6 us (100%)
    pallas_call x1, Pallas kernels, fast_body(): pl.pallas_call(functools.partial(gather_kernel, n, planes), out_shape=(ja...  47 us
    pallas_call x1, Pallas kernels, fast_body(): pl.pallas_call(project_kernel, out_shape=jax.ShapeDtypeStruct((batch, cl,...  4.61 us

commit v1 on v0

v1 whole, which is shorter than its diff:
```python
import functools
import math

import jax
import jax.numpy as jnp
from jax import lax
from jax.experimental import pallas as pl
from jax.experimental.pallas import tpu as pltpu
from jax.sharding import PartitionSpec as P

MESH = pl.DeviceIdType.MESH
NT = (((1,), (1,)), ((), ()))


def flip(index, other, bits):
    total = 0
    for bit in range(bits):
        a = (index // (1 << bit)) % 2
        b = (other // (1 << bit)) % 2
        total = total + (a + b - 2 * a * b) * (1 << bit)
    return total


def send_order(q):
    order = []
    for j in range(q):
        order += [("outer", j), ("near", j)] + ([("plane", j)] if j else [])
    return order + [("centre", j) for j in range(q)]


def gather_kernel(
    n, first_late,
    exc_hbm, val_ref, cond_hbm, scr_ref,
    condt_hbm, valt_hbm, field_hbm,
    condt_ref, valt_ref, field_ref, exc, exct, cond_all, val_all, scr_pair, scr_mixed,
    part, red, early, early_all, late, fld, fld_all,
    exc_sem, own_sem, out_sem, field_sem,
    cond_send, cond_recv, scr_send, scr_recv, va_send, va_recv, vo_send, vo_recv, vb_send, vb_recv,
    part_send, red_recv, early_send, early_recv, late_send, late_recv, fld_send, fld_recv,
):
    rows, cl = val_ref.shape[0], exc.shape[1]
    batch = exc.shape[0]
    q = n // 4
    qbits, bits = q.bit_length() - 1, n.bit_length() - 1
    blocks, bbits = 2 * q, q.bit_length()
    me = lax.axis_index("row")
    my_z, my_q = me // q, me % q
    half = my_z // 2
    outer = (my_z + 1 + half) % 2
    is_outer, is_centre = outer == 1, outer == 0
    mine = half * q + my_q

    exc_copy = pltpu.make_async_copy(exc_hbm, exc, exc_sem)
    exc_copy.start()
    own_val = pltpu.make_async_copy(val_ref, val_all.at[my_q, my_z], own_sem.at[0])
    own_val.start()
    own_scr = pltpu.make_async_copy(scr_ref, scr_pair.at[my_z % 2], own_sem.at[1])
    own_scr.start()
    pltpu.make_async_copy(
        cond_hbm.at[:, pl.ds(pl.multiple_of(me * cl, cl), cl)], cond_all.at[me], cond_recv.at[me]
    ).start()

    barrier = pltpu.get_barrier_semaphore()
    for k in range(1, n):
        pl.semaphore_signal(barrier, inc=1, device_id={"row": flip(me, k, bits)}, device_id_type=MESH)
    pl.semaphore_wait(barrier, n - 1)

    def remote(src, dst, send, recv, to):
        return pltpu.make_async_remote_copy(
            src_ref=src, dst_ref=dst, send_sem=send, recv_sem=recv,
            device_id={"row": to}, device_id_type=MESH,
        )

    def device(kind, j):
        z = {"outer": 3 * (1 - half), "centre": 2 - half, "near": flip(my_z, 1, 2), "plane": my_z}[kind]
        return z * q + flip(my_q, j, qbits)

    sent = []

    def send(*args):
        copy = remote(*args)
        copy.start()
        sent.append(copy)

    send(val_ref, val_all.at[my_q, my_z], va_send.at[0], va_recv.at[my_z], device("centre", 0))
    send(val_ref, val_all.at[my_q, my_z], va_send.at[1], va_recv.at[my_z], device("near", 0))
    for at, (kind, j) in enumerate(send_order(q)):
        to = device(kind, j)
        send(
            cond_hbm.at[:, pl.ds(pl.multiple_of(to * cl, cl), cl)], cond_all.at[me],
            cond_send.at[at], cond_recv.at[me], to,
        )

    scr_copy = remote(scr_ref, scr_pair.at[my_z % 2], scr_send, scr_recv, device("near", 0))

    @pl.when(is_outer)
    def _():
        scr_copy.start()

    exc_copy.wait()

    def turn(b, carry):
        exct[pl.ds(pl.multiple_of(b * 128, 128), 128), :] = exc[b].T
        return carry

    lax.fori_loop(0, batch, turn, 0)

    own_val.wait()
    near_z = flip(my_z, 1, 2)
    far_z = 2 * (1 - half)
    pltpu.make_async_copy(val_ref, val_all.at[my_q, near_z], va_recv.at[near_z]).wait()
    over = remote(
        val_all.at[my_q, pl.ds(far_z, 2)], val_all.at[my_q, pl.ds(far_z, 2)], vo_send, vo_recv, device("near", 0)
    )

    @pl.when(is_centre)
    def _():
        for i in range(2):
            pltpu.make_async_copy(val_ref, val_all.at[my_q, far_z + i], va_recv.at[far_z + i]).wait()
        over.start()

    @pl.when(is_outer)
    def _():
        over.wait_recv()

    for k in range(1, q):
        send(val_all.at[my_q], val_all.at[my_q], vb_send.at[k], vb_recv.at[my_q], device("plane", k))
    for k in range(1, q):
        other = flip(my_q, k, qbits)
        pltpu.make_async_copy(val_all.at[other], val_all.at[other], vb_recv.at[other]).wait()

    def place(step):
        cross, j = (step // q + outer) % 2, step % q
        hh, qq = (half + cross) % 2, flip(my_q, j, qbits)
        direct = jnp.where((outer == 0) & (cross == 1) & (j >= first_late), 1, 0)
        return hh, qq, j, direct

    def to_reducer(step, block):
        return remote(part.at[step], red.at[me], part_send.at[step], red_recv.at[me], q + block)

    def to_centre(step, j, k):
        return remote(
            part.at[step], late.at[mine, j - first_late], late_send.at[j - first_late, k],
            late_recv.at[mine, j - first_late], q + flip(mine, k, bbits),
        )

    def group(step, carry):
        hh, qq, j, direct = place(step)
        block = hh * q + qq
        lanes = pl.ds(pl.multiple_of(block * 2 * rows, 2 * rows), 2 * rows)
        first = 2 * hh * q + qq
        for i in range(2):
            pltpu.make_async_copy(
                cond_all.at[first + i * q], cond_all.at[first + i * q], cond_recv.at[first + i * q]
            ).wait()
        cond = jnp.concatenate([cond_all[first], cond_all[first + q]], axis=0)
        vals = val_all[qq, pl.ds(2 * hh, 2)].reshape(2 * rows, val_ref.shape[1])
        valt = vals.astype(jnp.float32).T
        valt_ref[:, lanes] = valt.astype(jnp.bfloat16)
        mixed = lax.dot_general(exct[...], cond, NT, preferred_element_type=jnp.float32)
        summed = jnp.sum(mixed.reshape(batch, valt.shape[0], 2 * rows) * valt[None], axis=1)
        part[step] = summed.astype(part.dtype)

        @pl.when((direct == 0) & (q + block != me))
        def _():
            to_reducer(step, block).start()

        @pl.when((direct == 0) & (q + block == me))
        def _():
            red[me] = summed.astype(red.dtype)

        @pl.when(direct == 1)
        def _():
            for k in range(1, blocks):
                to_centre(step, j, k).start()
            late[mine, j - first_late] = summed.astype(late.dtype)

        condt_ref[:, lanes] = cond.T
        pltpu.make_async_copy(condt_ref.at[:, lanes], condt_hbm.at[:, lanes], out_sem.at[step, 0]).start()
        pltpu.make_async_copy(valt_ref.at[:, lanes], valt_hbm.at[:, lanes], out_sem.at[step, 1]).start()
        return carry

    lax.fori_loop(0, q, group, 0)
    own_scr.wait()

    @pl.when(is_centre)
    def _():
        other = 1 - my_z % 2
        pltpu.make_async_copy(scr_pair.at[other], scr_pair.at[other], scr_recv).wait()
        whole = scr_pair[...].reshape(2 * rows, scr_ref.shape[1]).astype(jnp.float32)
        for h in range(2):
            for i in range(q):
                first = 2 * h * q + i
                pieces = [whole[:, d * rows:(d + 1) * rows] for d in (first, first + q)]
                at = (h * q + i) * 2 * rows
                scr_mixed[:, at:at + 2 * rows] = jnp.concatenate(pieces, axis=1).astype(jnp.bfloat16)

    lax.fori_loop(q, 2 * q - 1, group, 0)

    def early_copy(k):
        return remote(
            early, early_all.at[mine], early_send.at[k], early_recv.at[mine], q + flip(mine, k, bbits)
        )

    @pl.when(is_centre)
    def _():
        own_outer, own_centre = 3 * half * q, (1 + half) * q
        far_outer, far_centre = 3 * (1 - half) * q, (2 - half) * q
        total = red[me].astype(jnp.float32)
        others = [(own_outer, j) for j in range(q)] + [(own_centre, j) for j in range(1, q)]
        others += [(far_outer, j) for j in range(q)] + [(far_centre, j) for j in range(first_late)]
        for base, j in others:
            other = base + flip(my_q, j, qbits)
            pltpu.make_async_copy(red.at[other], red.at[other], red_recv.at[other]).wait()
            total = total + red[other].astype(jnp.float32)
        early[...] = total.astype(early.dtype)
        early_all[mine] = total.astype(early.dtype)
        for k in range(1, blocks):
            early_copy(k).start()

    group(2 * q - 1, 0)

    def field_copy_to(k):
        return remote(fld, fld_all.at[mine], fld_send.at[k], fld_recv.at[mine], flip(me, k, bits))

    @pl.when(is_centre)
    def _():
        for k in range(1, blocks):
            other = flip(mine, k, bbits)
            pltpu.make_async_copy(early_all.at[other], early_all.at[other], early_recv.at[other]).wait()
        for i in range(q - first_late):
            for k in range(1, blocks):
                other = flip(mine, k, bbits)
                pltpu.make_async_copy(late.at[other, i], late.at[other, i], late_recv.at[other, i]).wait()
        dens = []
        for block in range(blocks):
            total = early_all[block].astype(jnp.float32)
            for j in range(first_late, q):
                source = (1 - block // q) * q + flip(block % q, j, qbits)
                total = total + late[source, j - first_late].astype(jnp.float32)
            dens.append(total)
        whole = jnp.concatenate(dens, axis=1).astype(jnp.bfloat16)
        got = lax.dot_general(whole, scr_mixed[...], NT, preferred_element_type=jnp.float32).astype(jnp.bfloat16)
        fld[...] = got
        fld_all[mine] = got
        for k in range(n - 1, 0, -1):
            field_copy_to(k).start()

    for k in range(1, blocks):
        other = flip(mine, k, bbits)
        pltpu.make_async_copy(fld_all.at[other], fld_all.at[other], fld_recv.at[other]).wait()

    @pl.when(is_outer)
    def _():
        pltpu.make_async_copy(fld_all.at[mine], fld_all.at[mine], fld_recv.at[mine]).wait()

    for block in range(blocks):
        field_ref[:, block * 2 * rows:(block + 1) * 2 * rows] = fld_all[block].astype(jnp.float32)
    field_copy = pltpu.make_async_copy(field_ref, field_hbm, field_sem)
    field_copy.start()

    def finish(step, carry):
        hh, qq, j, direct = place(step)
        block = hh * q + qq
        lanes = pl.ds(pl.multiple_of(block * 2 * rows, 2 * rows), 2 * rows)
        pltpu.make_async_copy(condt_ref.at[:, lanes], condt_hbm.at[:, lanes], out_sem.at[step, 0]).wait()
        pltpu.make_async_copy(valt_ref.at[:, lanes], valt_hbm.at[:, lanes], out_sem.at[step, 1]).wait()

        @pl.when((direct == 0) & (q + block != me))
        def _():
            to_reducer(step, block).wait_send()

        @pl.when(direct == 1)
        def _():
            for k in range(1, blocks):
                to_centre(step, j, k).wait_send()

        return carry

    lax.fori_loop(0, 2 * q, finish, 0)
    for copy in sent:
        copy.wait_send()

    @pl.when(is_outer)
    def _():
        scr_copy.wait_send()

    @pl.when(is_centre)
    def _():
        over.wait_send()
        for k in range(1, blocks):
            early_copy(k).wait_send()
        for k in range(1, n):
            field_copy_to(k).wait_send()

    field_copy.wait()


def project_kernel(condt_hbm, valt_hbm, field_hbm, out_hbm, condt_ref, valt_ref, field_ref, held, in_sem, out_sem):
    loads = [
        pltpu.make_async_copy(src, dst, in_sem.at[at])
        for at, (src, dst) in enumerate(((valt_hbm, valt_ref), (field_hbm, field_ref), (condt_hbm, condt_ref)))
    ]
    for load in loads:
        load.start()
    loads[0].wait()
    loads[1].wait()
    v = valt_ref.shape[0]
    batch = field_ref.shape[0]
    valt = valt_ref[...]
    copies = []
    for b in range(0, batch, 4):
        weights = jnp.concatenate(
            [valt * field_ref[b + i:b + i + 1, :].astype(jnp.bfloat16) for i in range(4)], axis=0
        )
        if b == 0:
            loads[2].wait()
        summed = lax.dot_general(condt_ref[...], weights, NT, preferred_element_type=jnp.float32)
        for i in range(4):
            held[b + i] = summed[:, i * v:(i + 1) * v].astype(jnp.bfloat16)
        copy = pltpu.make_async_copy(held.at[pl.ds(b, 4)], out_hbm.at[pl.ds(b, 4)], out_sem.at[b // 4])
        copy.start()
        copies.append(copy)
    for copy in copies:
        copy.wait()


def fast_body(n, excitations, valence_orb, conduction_orb, screened):
    batch, cl, v = excitations.shape
    rows, points = screened.shape
    q, first_late = n // 4, 1
    blocks, lates = 2 * q, q - first_late
    bf, f32, sent_as = jnp.bfloat16, jnp.float32, jnp.float32
    hbm = pl.BlockSpec(memory_space=pltpu.HBM)
    dma = pltpu.SemaphoreType.DMA
    condt, valt, field = pl.pallas_call(
        functools.partial(gather_kernel, n, first_late),
        out_shape=(
            jax.ShapeDtypeStruct((cl, points), bf),
            jax.ShapeDtypeStruct((v, points), bf),
            jax.ShapeDtypeStruct((batch, points), f32),
        ),
        in_specs=[hbm, hbm, hbm, hbm],
        out_specs=(hbm, hbm, hbm),
        scratch_shapes=[
            pltpu.VMEM((cl, points), bf),
            pltpu.VMEM((v, points), bf),
            pltpu.VMEM((batch, points), f32),
            pltpu.VMEM((batch, cl, v), bf),
            pltpu.VMEM((batch * v, cl), bf),
            pltpu.VMEM((n, rows, cl), bf),
            pltpu.VMEM((q, 4, rows, v), bf),
            pltpu.VMEM((2, rows, points), bf),
            pltpu.VMEM((2 * rows, points), bf),
            pltpu.VMEM((blocks, batch, 2 * rows), sent_as),
            pltpu.VMEM((n, batch, 2 * rows), sent_as),
            pltpu.VMEM((batch, 2 * rows), sent_as),
            pltpu.VMEM((blocks, batch, 2 * rows), sent_as),
            pltpu.VMEM((blocks, lates, batch, 2 * rows), sent_as),
            pltpu.VMEM((batch, 2 * rows), bf),
            pltpu.VMEM((blocks, batch, 2 * rows), bf),
            dma, dma((2,)), dma((blocks, 2)), dma,
            dma((n,)), dma((n,)), dma, dma, dma((2,)), dma((4,)), dma, dma, dma((q,)), dma((q,)),
            dma((blocks,)), dma((n,)), dma((blocks,)), dma((blocks,)),
            dma((lates, blocks)), dma((blocks, lates)), dma((n,)), dma((blocks,)),
        ],
        compiler_params=pltpu.CompilerParams(
            collective_id=0, has_side_effects=True, vmem_limit_bytes=63 * 1024 * 1024
        ),
        name="gather_field",
    )(excitations, valence_orb, conduction_orb, screened)
    return pl.pallas_call(
        project_kernel,
        out_shape=jax.ShapeDtypeStruct((batch, cl, v), bf),
        in_specs=[hbm, hbm, hbm],
        out_specs=hbm,
        scratch_shapes=[
            pltpu.VMEM((cl, points), bf), pltpu.VMEM((v, points), bf), pltpu.VMEM((batch, points), f32),
            pltpu.VMEM((batch, cl, v), bf), dma((3,)), dma((batch // 2,))],
        compiler_params=pltpu.CompilerParams(vmem_limit_bytes=63 * 1024 * 1024),
        name="project",
    )(condt, valt, field)


def over_blocks(total_rows, step_fn, initial):
    span_size = math.gcd(total_rows, 2048)
    block_count = total_rows // span_size
    if block_count == 1:
        return step_fn(initial, 0, span_size)
    return lax.fori_loop(
        0, block_count, lambda index, carry: step_fn(carry, index * span_size, span_size), initial
    )


def density_rows(flat_exc, batch, valence_rows, cond_rows):
    total_rows = valence_rows.shape[0]
    cond_local = cond_rows.shape[1]
    initial = jnp.zeros((batch, total_rows), jnp.float32)

    def step_fn(carry, offset, span_size):
        val_block = lax.dynamic_slice_in_dim(valence_rows, offset, span_size, 0)
        cond_block = lax.dynamic_slice_in_dim(cond_rows, offset, span_size, 0)
        mixed = lax.dot_general(
            flat_exc, val_block, (((1,), (1,)), ((), ())), preferred_element_type=jnp.float32
        )
        mixed = mixed.reshape(batch, cond_local, span_size)
        summed = jnp.sum(mixed * cond_block.T.astype(jnp.float32)[None], axis=1)
        return lax.dynamic_update_slice_in_dim(carry, summed, offset, 1)

    return over_blocks(total_rows, step_fn, initial)


def projection(carry, valence_rows, cond_rows, field_cols):
    total_rows = valence_rows.shape[0]
    batch = field_cols.shape[0]
    cond_local = cond_rows.shape[1]

    def step_fn(inner, offset, span_size):
        val_block = lax.dynamic_slice_in_dim(valence_rows, offset, span_size, 0)
        cond_block = lax.dynamic_slice_in_dim(cond_rows, offset, span_size, 0)
        field_block = lax.dynamic_slice_in_dim(field_cols, offset, span_size, 1)
        pair = (
            cond_block.T.astype(jnp.float32)[None] * field_block.astype(jnp.float32)[:, None, :]
        ).astype(jnp.bfloat16)
        pair = pair.reshape(batch * cond_local, span_size)
        return inner + jnp.dot(pair, val_block, preferred_element_type=jnp.float32)

    return over_blocks(total_rows, step_fn, carry)


def general_body(excitations, valence_orb, conduction_orb, screened):
    batch, cond_local, valence = excitations.shape
    flat_exc = excitations.reshape(batch * cond_local, valence)
    valence_whole = lax.all_gather(valence_orb, "row", axis=0, tiled=True)
    cond_rows = lax.all_to_all(conduction_orb, "row", split_axis=1, concat_axis=0, tiled=True)
    partial_density = density_rows(flat_exc, batch, valence_whole, cond_rows)
    density_whole = lax.psum(partial_density, "row").astype(jnp.bfloat16)
    field_mine = lax.dot_general(
        density_whole, screened, (((1,), (1,)), ((), ())), preferred_element_type=jnp.float32
    ).astype(jnp.bfloat16)
    initial = jnp.zeros((batch * cond_local, valence), jnp.float32)
    summed = projection(
        initial, valence_whole, cond_rows, lax.all_gather(field_mine, "row", axis=1, tiled=True)
    )
    return summed.reshape(batch, cond_local, valence).astype(jnp.bfloat16)


def body(n, excitations, valence_orb, conduction_orb, screened):
    batch, cl, v = excitations.shape
    rows = valence_orb.shape[0]
    fits = n == 16 and cl % 128 == 0 and v == 128 and rows == 64 and batch == 16
    if fits:
        return fast_body(n, excitations, valence_orb, conduction_orb, screened)
    return general_body(excitations, valence_orb, conduction_orb, screened)


def solution(mesh):
    in_specs = (
        P("grp", "row", None),
        P(("grp", "row"), None),
        P(("grp", "row"), None),
        P(("grp", "row"), None),
    )
    out_specs = P("grp", "row", None)
    return jax.shard_map(
        functools.partial(body, mesh.shape["row"]),
        mesh=mesh, in_specs=in_specs, out_specs=out_specs, check_vma=False,
    )
```

time: 51.8 us -> 54 us (1.042)
  Pallas kernels: 51.6 us -> 53.9 us
    pallas_call x1, Pallas kernels: 47 us -> 49.3 us  [fast_body(): pl.pallas_call(functools.partial(gather_kernel, n, first_late), out_shape...]
where the time goes in v1:
time: 54 us; the launch traced here: 53.9 us
  Pallas kernels  53.9 us (100%)
    pallas_call x1, Pallas kernels, fast_body(): pl.pallas_call(functools.partial(gather_kernel, n, first_late), out_shape...  49.3 us
    pallas_call x1, Pallas kernels, fast_body(): pl.pallas_call(project_kernel, out_shape=jax.ShapeDtypeStruct((batch, cl,...  4.61 us

profile of v1, /device:TPU:0, one launch (start us, length us, event | category | flops | bytes accessed | tf_op | source)
XLA Modules:
  0.0 53.9 jit_solution(17590778226133772940)
XLA Ops:
  0.0 49.3 %gather_field.1 = (bf16[512,1024]{1,0:T(8,128)(2,1)}, bf16[128,1024]{1,0:T(8,128)(2,1)}, f32[16,1024]{1,0:T(8,128)}) custom-call(bf16[16,512,128]{2,1,0:T(8,128)(2,1)} %exc_hbm.1, bf16[64,128]{1,0:T(8,128)(2,1)} %val_ref.1, bf16[64,8192]{1,0:T(8,128)(2,1)} %cond_hbm.1, bf16[64,1024]{1,0:T(8,128)(2,1)} %scr_ref.1), custom_call_target="tpu_custom_call" | custom-call | tf_op jit(solution)/shard_map/gather_field/pallas_call | solution.py:336
  49.3 4.6 %project.1 = bf16[16,512,128]{2,1,0:T(8,128)(2,1)} custom-call(bf16[512,1024]{1,0:T(8,128)(2,1)} %get-tuple-element.8.condt_hbm, bf16[128,1024]{1,0:T(8,128)(2,1)} %get-tuple-element.9.valt_hbm, f32[16,1024]{1,0:T(8,128)} %get-tuple-element.10.field_hbm), custom_call_target="tpu_custom_call" | custom-call | tf_op jit(solution)/shard_map/project/pallas_call | solution.py:372

commit v2 on v1

--- a/solution.py
+++ b/solution.py
@@ -35,7 +35,7 @@
     condt_ref, valt_ref, field_ref, exc, exct, cond_all, val_all, scr_pair, scr_mixed,
     part, red, early, early_all, late, fld, fld_all,
     exc_sem, own_sem, out_sem, field_sem,
-    cond_send, cond_recv, scr_send, scr_recv, va_send, va_recv, vo_send, vo_recv, vb_send, vb_recv,
+    cond_send, cond_recv, scr_send, scr_recv, va_send, va_recv, vb_send, vb_recv,
     part_send, red_recv, early_send, early_recv, late_send, late_recv, fld_send, fld_recv,
 ):
     rows, cl = val_ref.shape[0], exc.shape[1]
@@ -82,8 +82,8 @@
         copy.start()
         sent.append(copy)
 
-    send(val_ref, val_all.at[my_q, my_z], va_send.at[0], va_recv.at[my_z], device("centre", 0))
-    send(val_ref, val_all.at[my_q, my_z], va_send.at[1], va_recv.at[my_z], device("near", 0))
+    for at, kind in enumerate(("outer", "centre", "near")):
+        send(val_ref, val_all.at[my_q, my_z], va_send.at[at], va_recv.at[my_z], device(kind, 0))
     for at, (kind, j) in enumerate(send_order(q)):
         to = device(kind, j)
         send(
@@ -106,23 +106,9 @@
     lax.fori_loop(0, batch, turn, 0)
 
     own_val.wait()
-    near_z = flip(my_z, 1, 2)
-    far_z = 2 * (1 - half)
-    pltpu.make_async_copy(val_ref, val_all.at[my_q, near_z], va_recv.at[near_z]).wait()
-    over = remote(
-        val_all.at[my_q, pl.ds(far_z, 2)], val_all.at[my_q, pl.ds(far_z, 2)], vo_send, vo_recv, device("near", 0)
-    )
-
-    @pl.when(is_centre)
-    def _():
-        for i in range(2):
-            pltpu.make_async_copy(val_ref, val_all.at[my_q, far_z + i], va_recv.at[far_z + i]).wait()
-        over.start()
-
-    @pl.when(is_outer)
-    def _():
-        over.wait_recv()
-
+    for k in range(1, 4):
+        z = flip(my_z, k, 2)
+        pltpu.make_async_copy(val_ref, val_all.at[my_q, z], va_recv.at[z]).wait()
     for k in range(1, q):
         send(val_all.at[my_q], val_all.at[my_q], vb_send.at[k], vb_recv.at[my_q], device("plane", k))
     for k in range(1, q):
@@ -287,7 +273,6 @@
 
     @pl.when(is_centre)
     def _():
-        over.wait_send()
         for k in range(1, blocks):
             early_copy(k).wait_send()
         for k in range(1, n):
@@ -360,7 +345,7 @@
             pltpu.VMEM((batch, 2 * rows), bf),
             pltpu.VMEM((blocks, batch, 2 * rows), bf),
             dma, dma((2,)), dma((blocks, 2)), dma,
-            dma((n,)), dma((n,)), dma, dma, dma((2,)), dma((4,)), dma, dma, dma((q,)), dma((q,)),
+            dma((n,)), dma((n,)), dma, dma, dma((3,)), dma((4,)), dma((q,)), dma((q,)),
             dma((blocks,)), dma((n,)), dma((blocks,)), dma((blocks,)),
             dma((lates, blocks)), dma((blocks, lates)), dma((n,)), dma((blocks,)),
         ],

time: 54 us -> 48 us (0.89)
  Pallas kernels: 53.9 us -> 47.9 us
    pallas_call x1, Pallas kernels: 49.3 us -> 43.3 us  [fast_body(): pl.pallas_call(functools.partial(gather_kernel, n, first_late), out_shape...]
where the time goes in v2:
time: 48 us; the launch traced here: 47.9 us
  Pallas kernels  47.9 us (100%)
    pallas_call x1, Pallas kernels, fast_body(): pl.pallas_call(functools.partial(gather_kernel, n, first_late), out_shape...  43.3 us
    pallas_call x1, Pallas kernels, fast_body(): pl.pallas_call(project_kernel, out_shape=jax.ShapeDtypeStruct((batch, cl,...  4.61 us

profile of v2, /device:TPU:0, one launch (start us, length us, event | category | flops | bytes accessed | tf_op | source)
XLA Modules:
  0.0 47.9 jit_solution(12959796505385546386)
XLA Ops:
  0.0 43.3 %gather_field.1 = (bf16[512,1024]{1,0:T(8,128)(2,1)}, bf16[128,1024]{1,0:T(8,128)(2,1)}, f32[16,1024]{1,0:T(8,128)}) custom-call(bf16[16,512,128]{2,1,0:T(8,128)(2,1)} %exc_hbm.1, bf16[64,128]{1,0:T(8,128)(2,1)} %val_ref.1, bf16[64,8192]{1,0:T(8,128)(2,1)} %cond_hbm.1, bf16[64,1024]{1,0:T(8,128)(2,1)} %scr_ref.1), custom_call_target="tpu_custom_call" | custom-call | tf_op jit(solution)/shard_map/gather_field/pallas_call | solution.py:321
  43.3 4.6 %project.1 = bf16[16,512,128]{2,1,0:T(8,128)(2,1)} custom-call(bf16[512,1024]{1,0:T(8,128)(2,1)} %get-tuple-element.8.condt_hbm, bf16[128,1024]{1,0:T(8,128)(2,1)} %get-tuple-element.9.valt_hbm, f32[16,1024]{1,0:T(8,128)} %get-tuple-element.10.field_hbm), custom_call_target="tpu_custom_call" | custom-call | tf_op jit(solution)/shard_map/project/pallas_call | solution.py:357

commit v3 on v2

--- a/solution.py
+++ b/solution.py
@@ -31,10 +31,9 @@
 def gather_kernel(
     n, first_late,
     exc_hbm, val_ref, cond_hbm, scr_ref,
-    condt_hbm, valt_hbm, field_hbm,
     condt_ref, valt_ref, field_ref, exc, exct, cond_all, val_all, scr_pair, scr_mixed,
     part, red, early, early_all, late, fld, fld_all,
-    exc_sem, own_sem, out_sem, field_sem,
+    exc_sem, own_sem,
     cond_send, cond_recv, scr_send, scr_recv, va_send, va_recv, vb_send, vb_recv,
     part_send, red_recv, early_send, early_recv, late_send, late_recv, fld_send, fld_recv,
 ):
@@ -162,8 +161,6 @@
             late[mine, j - first_late] = summed.astype(late.dtype)
 
         condt_ref[:, lanes] = cond.T
-        pltpu.make_async_copy(condt_ref.at[:, lanes], condt_hbm.at[:, lanes], out_sem.at[step, 0]).start()
-        pltpu.make_async_copy(valt_ref.at[:, lanes], valt_hbm.at[:, lanes], out_sem.at[step, 1]).start()
         return carry
 
     lax.fori_loop(0, q, group, 0)
@@ -242,15 +239,10 @@
 
     for block in range(blocks):
         field_ref[:, block * 2 * rows:(block + 1) * 2 * rows] = fld_all[block].astype(jnp.float32)
-    field_copy = pltpu.make_async_copy(field_ref, field_hbm, field_sem)
-    field_copy.start()
 
     def finish(step, carry):
         hh, qq, j, direct = place(step)
         block = hh * q + qq
-        lanes = pl.ds(pl.multiple_of(block * 2 * rows, 2 * rows), 2 * rows)
-        pltpu.make_async_copy(condt_ref.at[:, lanes], condt_hbm.at[:, lanes], out_sem.at[step, 0]).wait()
-        pltpu.make_async_copy(valt_ref.at[:, lanes], valt_hbm.at[:, lanes], out_sem.at[step, 1]).wait()
 
         @pl.when((direct == 0) & (q + block != me))
         def _():
@@ -278,18 +270,8 @@
         for k in range(1, n):
             field_copy_to(k).wait_send()
 
-    field_copy.wait()
-
-
-def project_kernel(condt_hbm, valt_hbm, field_hbm, out_hbm, condt_ref, valt_ref, field_ref, held, in_sem, out_sem):
-    loads = [
-        pltpu.make_async_copy(src, dst, in_sem.at[at])
-        for at, (src, dst) in enumerate(((valt_hbm, valt_ref), (field_hbm, field_ref), (condt_hbm, condt_ref)))
-    ]
-    for load in loads:
-        load.start()
-    loads[0].wait()
-    loads[1].wait()
+
+def project_kernel(condt_ref, valt_ref, field_ref, out_hbm, held, out_sem):
     v = valt_ref.shape[0]
     batch = field_ref.shape[0]
     valt = valt_ref[...]
@@ -298,8 +280,6 @@
         weights = jnp.concatenate(
             [valt * field_ref[b + i:b + i + 1, :].astype(jnp.bfloat16) for i in range(4)], axis=0
         )
-        if b == 0:
-            loads[2].wait()
         summed = lax.dot_general(condt_ref[...], weights, NT, preferred_element_type=jnp.float32)
         for i in range(4):
             held[b + i] = summed[:, i * v:(i + 1) * v].astype(jnp.bfloat16)
@@ -313,10 +293,11 @@
 def fast_body(n, excitations, valence_orb, conduction_orb, screened):
     batch, cl, v = excitations.shape
     rows, points = screened.shape
-    q, first_late = n // 4, 1
+    q, first_late = n // 4, 2
     blocks, lates = 2 * q, q - first_late
     bf, f32, sent_as = jnp.bfloat16, jnp.float32, jnp.float32
     hbm = pl.BlockSpec(memory_space=pltpu.HBM)
+    vmem = pl.BlockSpec(memory_space=pltpu.VMEM)
     dma = pltpu.SemaphoreType.DMA
     condt, valt, field = pl.pallas_call(
         functools.partial(gather_kernel, n, first_late),
@@ -326,11 +307,8 @@
             jax.ShapeDtypeStruct((batch, points), f32),
         ),
         in_specs=[hbm, hbm, hbm, hbm],
-        out_specs=(hbm, hbm, hbm),
+        out_specs=(vmem, vmem, vmem),
         scratch_shapes=[
-            pltpu.VMEM((cl, points), bf),
-            pltpu.VMEM((v, points), bf),
-            pltpu.VMEM((batch, points), f32),
             pltpu.VMEM((batch, cl, v), bf),
             pltpu.VMEM((batch * v, cl), bf),
             pltpu.VMEM((n, rows, cl), bf),
@@ -344,25 +322,23 @@
             pltpu.VMEM((blocks, lates, batch, 2 * rows), sent_as),
             pltpu.VMEM((batch, 2 * rows), bf),
             pltpu.VMEM((blocks, batch, 2 * rows), bf),
-            dma, dma((2,)), dma((blocks, 2)), dma,
+            dma, dma((2,)),
             dma((n,)), dma((n,)), dma, dma, dma((3,)), dma((4,)), dma((q,)), dma((q,)),
             dma((blocks,)), dma((n,)), dma((blocks,)), dma((blocks,)),
             dma((lates, blocks)), dma((blocks, lates)), dma((n,)), dma((blocks,)),
         ],
         compiler_params=pltpu.CompilerParams(
-            collective_id=0, has_side_effects=True, vmem_limit_bytes=63 * 1024 * 1024
+            collective_id=0, has_side_effects=True, vmem_limit_bytes=24 * 1024 * 1024
         ),
         name="gather_field",
-    )(excitations, valence_orb, conduction_orb, screened)
+    )(*[pltpu.with_memory_space_constraint(x, pltpu.HBM) for x in (excitations, valence_orb, conduction_orb, screened)])
     return pl.pallas_call(
         project_kernel,
         out_shape=jax.ShapeDtypeStruct((batch, cl, v), bf),
-        in_specs=[hbm, hbm, hbm],
+        in_specs=[vmem, vmem, vmem],
         out_specs=hbm,
-        scratch_shapes=[
-            pltpu.VMEM((cl, points), bf), pltpu.VMEM((v, points), bf), pltpu.VMEM((batch, points), f32),
-            pltpu.VMEM((batch, cl, v), bf), dma((3,)), dma((batch // 2,))],
-        compiler_params=pltpu.CompilerParams(vmem_limit_bytes=63 * 1024 * 1024),
+        scratch_shapes=[pltpu.VMEM((batch, cl, v), bf), dma((batch // 4,))],
+        compiler_params=pltpu.CompilerParams(vmem_limit_bytes=24 * 1024 * 1024),
         name="project",
     )(condt, valt, field)
 

time: 48 us -> 45.9 us (0.956)
  Pallas kernels: 47.9 us -> 45.8 us
    pallas_call x1, Pallas kernels: 4.61 us -> 3.2 us  [fast_body(): pl.pallas_call(project_kernel, out_shape=jax.ShapeDtypeStruct((batch, cl,...]
    pallas_call x1, Pallas kernels: 43.3 us -> 42.6 us  [fast_body(): pl.pallas_call(functools.partial(gather_kernel, n, first_late), out_shape...]
where the time goes in v3:
time: 45.9 us; the launch traced here: 45.8 us
  Pallas kernels  45.8 us (100%)
    pallas_call x1, Pallas kernels, fast_body(): pl.pallas_call(functools.partial(gather_kernel, n, first_late), out_shape...  42.6 us
    pallas_call x1, Pallas kernels, fast_body(): pl.pallas_call(project_kernel, out_shape=jax.ShapeDtypeStruct((batch, cl,...  3.2 us

profile of v3, /device:TPU:0, one launch (start us, length us, event | category | flops | bytes accessed | tf_op | source)
XLA Modules:
  0.0 45.8 jit_solution(5433995803695116888)
XLA Ops:
  0.0 42.6 %gather_field.1 = (bf16[512,1024]{1,0:T(8,128)(2,1)S(1)}, bf16[128,1024]{1,0:T(8,128)(2,1)S(1)}, f32[16,1024]{1,0:T(8,128)S(1)}) custom-call(bf16[16,512,128]{2,1,0:T(8,128)(2,1)} %exc_hbm.1, bf16[64,128]{1,0:T(8,128)(2,1)} %val_ref.1, bf16[64,8192]{1,0:T(8,128)(2,1)} %cond_hbm.1, bf16[64,1024]{1,0:T(8,128)(2,1)} %scr_ref.1), custom_call_target="tpu_custom_call" | custom-call | tf_op jit(solution)/shard_map/gather_field/pallas_call | solution.py:302
  42.6 3.2 %project.1 = bf16[16,512,128]{2,1,0:T(8,128)(2,1)} custom-call(bf16[512,1024]{1,0:T(8,128)(2,1)S(1)} %get-tuple-element.8.condt_ref, bf16[128,1024]{1,0:T(8,128)(2,1)S(1)} %get-tuple-element.9.valt_ref, f32[16,1024]{1,0:T(8,128)S(1)} %get-tuple-element.10.field_ref), custom_call_target="tpu_custom_call" | custom-call | tf_op jit(solution)/shard_map/project/pallas_call | solution.py:335

commit v4 on v3

--- a/solution.py
+++ b/solution.py
@@ -21,11 +21,7 @@
     return total
 
 
-def send_order(q):
-    order = []
-    for j in range(q):
-        order += [("outer", j), ("near", j)] + ([("plane", j)] if j else [])
-    return order + [("centre", j) for j in range(q)]
+KINDS = ("outer", "centre", "near", "plane")
 
 
 def gather_kernel(
@@ -49,6 +45,12 @@
     is_outer, is_centre = outer == 1, outer == 0
     mine = half * q + my_q
 
+    barrier = pltpu.get_barrier_semaphore()
+    for k in range(n - 1, 0, -1):
+        to = flip(me, k, bits)
+
+        pl.semaphore_signal(barrier, inc=1, device_id={"row": to}, device_id_type=MESH)
+
     exc_copy = pltpu.make_async_copy(exc_hbm, exc, exc_sem)
     exc_copy.start()
     own_val = pltpu.make_async_copy(val_ref, val_all.at[my_q, my_z], own_sem.at[0])
@@ -58,10 +60,6 @@
     pltpu.make_async_copy(
         cond_hbm.at[:, pl.ds(pl.multiple_of(me * cl, cl), cl)], cond_all.at[me], cond_recv.at[me]
     ).start()
-
-    barrier = pltpu.get_barrier_semaphore()
-    for k in range(1, n):
-        pl.semaphore_signal(barrier, inc=1, device_id={"row": flip(me, k, bits)}, device_id_type=MESH)
     pl.semaphore_wait(barrier, n - 1)
 
     def remote(src, dst, send, recv, to):
@@ -74,27 +72,24 @@
         z = {"outer": 3 * (1 - half), "centre": 2 - half, "near": flip(my_z, 1, 2), "plane": my_z}[kind]
         return z * q + flip(my_q, j, qbits)
 
-    sent = []
-
-    def send(*args):
-        copy = remote(*args)
-        copy.start()
-        sent.append(copy)
-
-    for at, kind in enumerate(("outer", "centre", "near")):
-        send(val_ref, val_all.at[my_q, my_z], va_send.at[at], va_recv.at[my_z], device(kind, 0))
-    for at, (kind, j) in enumerate(send_order(q)):
+    def block_to(kind, j):
         to = device(kind, j)
-        send(
+        return remote(
             cond_hbm.at[:, pl.ds(pl.multiple_of(to * cl, cl), cl)], cond_all.at[me],
-            cond_send.at[at], cond_recv.at[me], to,
-        )
+            cond_send.at[KINDS.index(kind) * q + j], cond_recv.at[me], to,
+        )
+
+    def val_to(at, kind):
+        return remote(val_ref, val_all.at[my_q, my_z], va_send.at[at], va_recv.at[my_z], device(kind, 0))
 
     scr_copy = remote(scr_ref, scr_pair.at[my_z % 2], scr_send, scr_recv, device("near", 0))
 
-    @pl.when(is_outer)
-    def _():
-        scr_copy.start()
+    val_to(0, "outer").start()
+    val_to(1, "centre").start()
+    val_to(2, "near").start()
+    for j in range(q):
+        block_to("outer", j).start()
+
 
     exc_copy.wait()
 
@@ -105,11 +100,30 @@
     lax.fori_loop(0, batch, turn, 0)
 
     own_val.wait()
+    def val_wait(z):
+        pltpu.make_async_copy(val_ref, val_all.at[my_q, z], va_recv.at[z]).wait()
+
+    def share(k):
+        return remote(val_all.at[my_q], val_all.at[my_q], vb_send.at[k], vb_recv.at[my_q], device("plane", k))
+
     for k in range(1, 4):
-        z = flip(my_z, k, 2)
-        pltpu.make_async_copy(val_ref, val_all.at[my_q, z], va_recv.at[z]).wait()
+        val_wait(flip(my_z, k, 2))
     for k in range(1, q):
-        send(val_all.at[my_q], val_all.at[my_q], vb_send.at[k], vb_recv.at[my_q], device("plane", k))
+        share(k).start()
+    for j in range(1, q):
+        block_to("plane", j).start()
+    for j in range(q):
+        block_to("near", j).start()
+
+    @pl.when(is_centre)
+    def _():
+        for j in range(q):
+            block_to("centre", j).start()
+
+    @pl.when(is_outer)
+    def _():
+        scr_copy.start()
+
     for k in range(1, q):
         other = flip(my_q, k, qbits)
         pltpu.make_async_copy(val_all.at[other], val_all.at[other], vb_recv.at[other]).wait()
@@ -164,6 +178,11 @@
         return carry
 
     lax.fori_loop(0, q, group, 0)
+    @pl.when(is_outer)
+    def _():
+        for j in range(q):
+            block_to("centre", j).start()
+
     own_scr.wait()
 
     @pl.when(is_centre)
@@ -176,7 +195,7 @@
                 first = 2 * h * q + i
                 pieces = [whole[:, d * rows:(d + 1) * rows] for d in (first, first + q)]
                 at = (h * q + i) * 2 * rows
-                scr_mixed[:, at:at + 2 * rows] = jnp.concatenate(pieces, axis=1).astype(jnp.bfloat16)
+                scr_mixed[at:at + 2 * rows, :] = jnp.concatenate(pieces, axis=1).T.astype(jnp.bfloat16)
 
     lax.fori_loop(q, 2 * q - 1, group, 0)
 
@@ -223,7 +242,7 @@
                 total = total + late[source, j - first_late].astype(jnp.float32)
             dens.append(total)
         whole = jnp.concatenate(dens, axis=1).astype(jnp.bfloat16)
-        got = lax.dot_general(whole, scr_mixed[...], NT, preferred_element_type=jnp.float32).astype(jnp.bfloat16)
+        got = jnp.dot(whole, scr_mixed[...], preferred_element_type=jnp.float32).astype(jnp.bfloat16)
         fld[...] = got
         fld_all[mine] = got
         for k in range(n - 1, 0, -1):
@@ -256,8 +275,13 @@
         return carry
 
     lax.fori_loop(0, 2 * q, finish, 0)
-    for copy in sent:
-        copy.wait_send()
+    for kind in KINDS:
+        for j in range(1 if kind == "plane" else 0, q):
+            block_to(kind, j).wait_send()
+    for at, kind in enumerate(("outer", "centre", "near")):
+        val_to(at, kind).wait_send()
+    for k in range(1, q):
+        share(k).wait_send()
 
     @pl.when(is_outer)
     def _():
@@ -295,7 +319,7 @@
     rows, points = screened.shape
     q, first_late = n // 4, 2
     blocks, lates = 2 * q, q - first_late
-    bf, f32, sent_as = jnp.bfloat16, jnp.float32, jnp.float32
+    bf, f32, sent_as = jnp.bfloat16, jnp.float32, jnp.bfloat16
     hbm = pl.BlockSpec(memory_space=pltpu.HBM)
     vmem = pl.BlockSpec(memory_space=pltpu.VMEM)
     dma = pltpu.SemaphoreType.DMA
@@ -314,11 +338,11 @@
             pltpu.VMEM((n, rows, cl), bf),
             pltpu.VMEM((q, 4, rows, v), bf),
             pltpu.VMEM((2, rows, points), bf),
-            pltpu.VMEM((2 * rows, points), bf),
+            pltpu.VMEM((points, 2 * rows), bf),
             pltpu.VMEM((blocks, batch, 2 * rows), sent_as),
             pltpu.VMEM((n, batch, 2 * rows), sent_as),
-            pltpu.VMEM((batch, 2 * rows), sent_as),
-            pltpu.VMEM((blocks, batch, 2 * rows), sent_as),
+            pltpu.VMEM((batch, 2 * rows), f32),
+            pltpu.VMEM((blocks, batch, 2 * rows), f32),
             pltpu.VMEM((blocks, lates, batch, 2 * rows), sent_as),
             pltpu.VMEM((batch, 2 * rows), bf),
             pltpu.VMEM((blocks, batch, 2 * rows), bf),

time: 45.9 us -> 44.8 us (0.976)
  Pallas kernels: 45.8 us -> 44.6 us
    pallas_call x1, Pallas kernels: 42.6 us -> 41.4 us  [fast_body(): pl.pallas_call(functools.partial(gather_kernel, n, first_late), out_shape...]
where the time goes in v4:
time: 44.8 us; the launch traced here: 44.6 us
  Pallas kernels  44.6 us (100%)
    pallas_call x1, Pallas kernels, fast_body(): pl.pallas_call(functools.partial(gather_kernel, n, first_late), out_shape...  41.4 us
    pallas_call x1, Pallas kernels, fast_body(): pl.pallas_call(project_kernel, out_shape=jax.ShapeDtypeStruct((batch, cl,...  3.2 us

profile of v4, /device:TPU:0, one launch (start us, length us, event | category | flops | bytes accessed | tf_op | source)
XLA Modules:
  0.0 44.6 jit_solution(14327600971729458211)
XLA Ops:
  0.0 41.4 %gather_field.1 = (bf16[512,1024]{1,0:T(8,128)(2,1)S(1)}, bf16[128,1024]{1,0:T(8,128)(2,1)S(1)}, f32[16,1024]{1,0:T(8,128)S(1)}) custom-call(bf16[16,512,128]{2,1,0:T(8,128)(2,1)} %exc_hbm.1, bf16[64,128]{1,0:T(8,128)(2,1)} %val_ref.1, bf16[64,8192]{1,0:T(8,128)(2,1)} %cond_hbm.1, bf16[64,1024]{1,0:T(8,128)(2,1)} %scr_ref.1), custom_call_target="tpu_custom_call" | custom-call | tf_op jit(solution)/shard_map/gather_field/pallas_call | solution.py:326
  41.4 3.2 %project.1 = bf16[16,512,128]{2,1,0:T(8,128)(2,1)} custom-call(bf16[512,1024]{1,0:T(8,128)(2,1)S(1)} %get-tuple-element.8.condt_ref, bf16[128,1024]{1,0:T(8,128)(2,1)S(1)} %get-tuple-element.9.valt_ref, f32[16,1024]{1,0:T(8,128)S(1)} %get-tuple-element.10.field_ref), custom_call_target="tpu_custom_call" | custom-call | tf_op jit(solution)/shard_map/project/pallas_call | solution.py:359

commit v5 on v4

--- a/solution.py
+++ b/solution.py
@@ -170,18 +170,19 @@
 
         @pl.when(direct == 1)
         def _():
-            for k in range(1, blocks):
+            for k in range(blocks - 1, 0, -1):
                 to_centre(step, j, k).start()
             late[mine, j - first_late] = summed.astype(late.dtype)
 
         condt_ref[:, lanes] = cond.T
+
+        @pl.when((outer == 1) & (step < q))
+        def _():
+            block_to("centre", step).start()
+
         return carry
 
     lax.fori_loop(0, q, group, 0)
-    @pl.when(is_outer)
-    def _():
-        for j in range(q):
-            block_to("centre", j).start()
 
     own_scr.wait()
 
@@ -217,36 +218,36 @@
             total = total + red[other].astype(jnp.float32)
         early[...] = total.astype(early.dtype)
         early_all[mine] = total.astype(early.dtype)
-        for k in range(1, blocks):
+        for k in range(blocks - 1, 0, -1):
             early_copy(k).start()
 
     group(2 * q - 1, 0)
 
     def field_copy_to(k):
-        return remote(fld, fld_all.at[mine], fld_send.at[k], fld_recv.at[mine], flip(me, k, bits))
+        return remote(fld, fld_all.at[mine], fld_send.at[k], fld_recv.at[mine], k)
 
     @pl.when(is_centre)
     def _():
         for k in range(1, blocks):
             other = flip(mine, k, bbits)
             pltpu.make_async_copy(early_all.at[other], early_all.at[other], early_recv.at[other]).wait()
-        for i in range(q - first_late):
+        dens = [early_all[block].astype(jnp.float32) for block in range(blocks)]
+        for j in range(first_late, q):
+            at = j - first_late
             for k in range(1, blocks):
                 other = flip(mine, k, bbits)
-                pltpu.make_async_copy(late.at[other, i], late.at[other, i], late_recv.at[other, i]).wait()
-        dens = []
-        for block in range(blocks):
-            total = early_all[block].astype(jnp.float32)
-            for j in range(first_late, q):
+                pltpu.make_async_copy(late.at[other, at], late.at[other, at], late_recv.at[other, at]).wait()
+            for block in range(blocks):
                 source = (1 - block // q) * q + flip(block % q, j, qbits)
-                total = total + late[source, j - first_late].astype(jnp.float32)
-            dens.append(total)
+                dens[block] = dens[block] + late[source, at].astype(jnp.float32)
         whole = jnp.concatenate(dens, axis=1).astype(jnp.bfloat16)
         got = jnp.dot(whole, scr_mixed[...], preferred_element_type=jnp.float32).astype(jnp.bfloat16)
         fld[...] = got
         fld_all[mine] = got
-        for k in range(n - 1, 0, -1):
-            field_copy_to(k).start()
+        for to in [*range(q), *range(3 * q, n), *range(2 * q, 3 * q), *range(q, 2 * q)]:
+            @pl.when(to != me)
+            def _():
+                field_copy_to(to).start()
 
     for k in range(1, blocks):
         other = flip(mine, k, bbits)
@@ -291,8 +292,10 @@
     def _():
         for k in range(1, blocks):
             early_copy(k).wait_send()
-        for k in range(1, n):
-            field_copy_to(k).wait_send()
+        for to in range(n):
+            @pl.when(to != me)
+            def _():
+                field_copy_to(to).wait_send()
 
 
 def project_kernel(condt_ref, valt_ref, field_ref, out_hbm, held, out_sem):

time: 44.8 us -> 44.7 us (level)
  no operation moved by 1% of the time
where the time goes in v5:
time: 44.7 us; the launch traced here: 44.6 us
  Pallas kernels  44.6 us (100%)
    pallas_call x1, Pallas kernels, fast_body(): pl.pallas_call(functools.partial(gather_kernel, n, first_late), out_shape...  41.4 us
    pallas_call x1, Pallas kernels, fast_body(): pl.pallas_call(project_kernel, out_shape=jax.ShapeDtypeStruct((batch, cl,...  3.2 us

profile of v5, /device:TPU:0, one launch (start us, length us, event | category | flops | bytes accessed | tf_op | source)
XLA Modules:
  0.0 44.6 jit_solution(2635807724159446155)
XLA Ops:
  0.0 41.4 %gather_field.1 = (bf16[512,1024]{1,0:T(8,128)(2,1)S(1)}, bf16[128,1024]{1,0:T(8,128)(2,1)S(1)}, f32[16,1024]{1,0:T(8,128)S(1)}) custom-call(bf16[16,512,128]{2,1,0:T(8,128)(2,1)} %exc_hbm.1, bf16[64,128]{1,0:T(8,128)(2,1)} %val_ref.1, bf16[64,8192]{1,0:T(8,128)(2,1)} %cond_hbm.1, bf16[64,1024]{1,0:T(8,128)(2,1)} %scr_ref.1), custom_call_target="tpu_custom_call" | custom-call | tf_op jit(solution)/shard_map/gather_field/pallas_call | solution.py:329
  41.4 3.2 %project.1 = bf16[16,512,128]{2,1,0:T(8,128)(2,1)} custom-call(bf16[512,1024]{1,0:T(8,128)(2,1)S(1)} %get-tuple-element.8.condt_ref, bf16[128,1024]{1,0:T(8,128)(2,1)S(1)} %get-tuple-element.9.valt_ref, f32[16,1024]{1,0:T(8,128)S(1)} %get-tuple-element.10.field_ref), custom_call_target="tpu_custom_call" | custom-call | tf_op jit(solution)/shard_map/project/pallas_call | solution.py:362

commit v6 on v5

--- a/solution.py
+++ b/solution.py
@@ -28,7 +28,7 @@
     n, first_late,
     exc_hbm, val_ref, cond_hbm, scr_ref,
     condt_ref, valt_ref, field_ref, exc, exct, cond_all, val_all, scr_pair, scr_mixed,
-    part, red, early, early_all, late, fld, fld_all,
+    part, tail, red, early, early_all, late, fld, fld_all,
     exc_sem, own_sem,
     cond_send, cond_recv, scr_send, scr_recv, va_send, va_recv, vb_send, vb_recv,
     part_send, red_recv, early_send, early_recv, late_send, late_recv, fld_send, fld_recv,
@@ -139,7 +139,7 @@
 
     def to_centre(step, j, k):
         return remote(
-            part.at[step], late.at[mine, j - first_late], late_send.at[j - first_late, k],
+            tail.at[j - first_late], late.at[mine, j - first_late], late_send.at[j - first_late, k],
             late_recv.at[mine, j - first_late], q + flip(mine, k, bbits),
         )
 
@@ -170,6 +170,7 @@
 
         @pl.when(direct == 1)
         def _():
+            tail[j - first_late] = summed.astype(tail.dtype)
             for k in range(blocks - 1, 0, -1):
                 to_centre(step, j, k).start()
             late[mine, j - first_late] = summed.astype(late.dtype)
@@ -322,7 +323,7 @@
     rows, points = screened.shape
     q, first_late = n // 4, 2
     blocks, lates = 2 * q, q - first_late
-    bf, f32, sent_as = jnp.bfloat16, jnp.float32, jnp.bfloat16
+    bf, f32 = jnp.bfloat16, jnp.float32
     hbm = pl.BlockSpec(memory_space=pltpu.HBM)
     vmem = pl.BlockSpec(memory_space=pltpu.VMEM)
     dma = pltpu.SemaphoreType.DMA
@@ -342,11 +343,12 @@
             pltpu.VMEM((q, 4, rows, v), bf),
             pltpu.VMEM((2, rows, points), bf),
             pltpu.VMEM((points, 2 * rows), bf),
-            pltpu.VMEM((blocks, batch, 2 * rows), sent_as),
-            pltpu.VMEM((n, batch, 2 * rows), sent_as),
+            pltpu.VMEM((blocks, batch, 2 * rows), bf),
+            pltpu.VMEM((lates, batch, 2 * rows), f32),
+            pltpu.VMEM((n, batch, 2 * rows), bf),
             pltpu.VMEM((batch, 2 * rows), f32),
             pltpu.VMEM((blocks, batch, 2 * rows), f32),
-            pltpu.VMEM((blocks, lates, batch, 2 * rows), sent_as),
+            pltpu.VMEM((blocks, lates, batch, 2 * rows), f32),
             pltpu.VMEM((batch, 2 * rows), bf),
             pltpu.VMEM((blocks, batch, 2 * rows), bf),
             dma, dma((2,)),

time: 44.7 us -> 44.8 us (level)
  no operation moved by 1% of the time
where the time goes in v6:
time: 44.8 us; the launch traced here: 44.7 us
  Pallas kernels  44.7 us (100%)
    pallas_call x1, Pallas kernels, fast_body(): pl.pallas_call(functools.partial(gather_kernel, n, first_late), out_shape...  41.5 us
    pallas_call x1, Pallas kernels, fast_body(): pl.pallas_call(project_kernel, out_shape=jax.ShapeDtypeStruct((batch, cl,...  3.2 us

profile of v6, /device:TPU:0, one launch (start us, length us, event | category | flops | bytes accessed | tf_op | source)
XLA Modules:
  0.0 44.7 jit_solution(8113404955458896508)
XLA Ops:
  0.0 41.5 %gather_field.1 = (bf16[512,1024]{1,0:T(8,128)(2,1)S(1)}, bf16[128,1024]{1,0:T(8,128)(2,1)S(1)}, f32[16,1024]{1,0:T(8,128)S(1)}) custom-call(bf16[16,512,128]{2,1,0:T(8,128)(2,1)} %exc_hbm.1, bf16[64,128]{1,0:T(8,128)(2,1)} %val_ref.1, bf16[64,8192]{1,0:T(8,128)(2,1)} %cond_hbm.1, bf16[64,1024]{1,0:T(8,128)(2,1)} %scr_ref.1), custom_call_target="tpu_custom_call" | custom-call | tf_op jit(solution)/shard_map/gather_field/pallas_call | solution.py:330
  41.5 3.2 %project.1 = bf16[16,512,128]{2,1,0:T(8,128)(2,1)} custom-call(bf16[512,1024]{1,0:T(8,128)(2,1)S(1)} %get-tuple-element.8.condt_ref, bf16[128,1024]{1,0:T(8,128)(2,1)S(1)} %get-tuple-element.9.valt_ref, f32[16,1024]{1,0:T(8,128)S(1)} %get-tuple-element.10.field_ref), custom_call_target="tpu_custom_call" | custom-call | tf_op jit(solution)/shard_map/project/pallas_call | solution.py:364

commit v7 on v5

--- a/solution.py
+++ b/solution.py
@@ -87,8 +87,7 @@
     val_to(0, "outer").start()
     val_to(1, "centre").start()
     val_to(2, "near").start()
-    for j in range(q):
-        block_to("outer", j).start()
+    block_to("outer", 0).start()
 
 
     exc_copy.wait()
@@ -110,6 +109,8 @@
         val_wait(flip(my_z, k, 2))
     for k in range(1, q):
         share(k).start()
+    for j in range(1, q):
+        block_to("outer", j).start()
     for j in range(1, q):
         block_to("plane", j).start()
     for j in range(q):

time: 44.7 us -> 44.7 us (level)
  no operation moved by 1% of the time
where the time goes in v7:
time: 44.7 us; the launch traced here: 44.6 us
  Pallas kernels  44.6 us (100%)
    pallas_call x1, Pallas kernels, fast_body(): pl.pallas_call(functools.partial(gather_kernel, n, first_late), out_shape...  41.4 us
    pallas_call x1, Pallas kernels, fast_body(): pl.pallas_call(project_kernel, out_shape=jax.ShapeDtypeStruct((batch, cl,...  3.2 us

profile of v7, /device:TPU:0, one launch (start us, length us, event | category | flops | bytes accessed | tf_op | source)
XLA Modules:
  0.0 44.6 jit_solution(3981043372002269657)
XLA Ops:
  0.0 41.4 %gather_field.1 = (bf16[512,1024]{1,0:T(8,128)(2,1)S(1)}, bf16[128,1024]{1,0:T(8,128)(2,1)S(1)}, f32[16,1024]{1,0:T(8,128)S(1)}) custom-call(bf16[16,512,128]{2,1,0:T(8,128)(2,1)} %exc_hbm.1, bf16[64,128]{1,0:T(8,128)(2,1)} %val_ref.1, bf16[64,8192]{1,0:T(8,128)(2,1)} %cond_hbm.1, bf16[64,1024]{1,0:T(8,128)(2,1)} %scr_ref.1), custom_call_target="tpu_custom_call" | custom-call | tf_op jit(solution)/shard_map/gather_field/pallas_call | solution.py:330
  41.4 3.2 %project.1 = bf16[16,512,128]{2,1,0:T(8,128)(2,1)} custom-call(bf16[512,1024]{1,0:T(8,128)(2,1)S(1)} %get-tuple-element.8.condt_ref, bf16[128,1024]{1,0:T(8,128)(2,1)S(1)} %get-tuple-element.9.valt_ref, f32[16,1024]{1,0:T(8,128)S(1)} %get-tuple-element.10.field_ref), custom_call_target="tpu_custom_call" | custom-call | tf_op jit(solution)/shard_map/project/pallas_call | solution.py:363

commit v8 on v7

--- a/solution.py
+++ b/solution.py
@@ -46,7 +46,7 @@
     mine = half * q + my_q
 
     barrier = pltpu.get_barrier_semaphore()
-    for k in range(n - 1, 0, -1):
+    for k in [z * q + i for z in (2, 3, 1, 0) for i in range(q) if z or i]:
         to = flip(me, k, bits)
 
         pl.semaphore_signal(barrier, inc=1, device_id={"row": to}, device_id_type=MESH)

time: 44.7 us -> 44.7 us (level)
  no operation moved by 1% of the time
where the time goes in v8:
time: 44.7 us; the launch traced here: 44.5 us
  Pallas kernels  44.5 us (100%)
    pallas_call x1, Pallas kernels, fast_body(): pl.pallas_call(functools.partial(gather_kernel, n, first_late), out_shape...  41.3 us
    pallas_call x1, Pallas kernels, fast_body(): pl.pallas_call(project_kernel, out_shape=jax.ShapeDtypeStruct((batch, cl,...  3.21 us

profile of v8, /device:TPU:0, one launch (start us, length us, event | category | flops | bytes accessed | tf_op | source)
XLA Modules:
  0.0 44.5 jit_solution(11287882174942315034)
XLA Ops:
  0.0 41.3 %gather_field.1 = (bf16[512,1024]{1,0:T(8,128)(2,1)S(1)}, bf16[128,1024]{1,0:T(8,128)(2,1)S(1)}, f32[16,1024]{1,0:T(8,128)S(1)}) custom-call(bf16[16,512,128]{2,1,0:T(8,128)(2,1)} %exc_hbm.1, bf16[64,128]{1,0:T(8,128)(2,1)} %val_ref.1, bf16[64,8192]{1,0:T(8,128)(2,1)} %cond_hbm.1, bf16[64,1024]{1,0:T(8,128)(2,1)} %scr_ref.1), custom_call_target="tpu_custom_call" | custom-call | tf_op jit(solution)/shard_map/gather_field/pallas_call | solution.py:330
  41.3 3.2 %project.1 = bf16[16,512,128]{2,1,0:T(8,128)(2,1)} custom-call(bf16[512,1024]{1,0:T(8,128)(2,1)S(1)} %get-tuple-element.8.condt_ref, bf16[128,1024]{1,0:T(8,128)(2,1)S(1)} %get-tuple-element.9.valt_ref, f32[16,1024]{1,0:T(8,128)S(1)} %get-tuple-element.10.field_ref), custom_call_target="tpu_custom_call" | custom-call | tf_op jit(solution)/shard_map/project/pallas_call | solution.py:363
